TPU v7x, 128 devices: a whole 4x4x4 slice. The times are simulated.
128 devices in a mesh: rep: 8 (over z, core), pipe: 8 (over y_lo, x), tp: 2 (over y_hi).
Axes of the slice: x: 4, y: 4 (y_hi: 2, y_lo: 2; y = y_hi * 2 + y_lo), z: 4, core: 2. Of those that a mesh axis runs over, the one named last changes fastest.
Arguments:
- fwd_in: bfloat16 [8, 8, 256, 3072], P('rep', 'pipe', None, 'tp'), may hold values from -6 to 6
- bwd_in: bfloat16 [8, 8, 256, 3072], P('rep', 'pipe', None, 'tp'), may hold values from -6 to 6
- bwd_grad: bfloat16 [8, 8, 256, 3072], P('rep', 'pipe', None, 'tp'), may hold values from -18 to 18
- seg_fwd: int32 [8, 8, 256], P('rep', 'pipe'), may hold values from 0 to 3, never falling along the last dimension, each value on 1 to 128 neighbouring positions
- seg_bwd: int32 [8, 8, 256], P('rep', 'pipe'), may hold values from 0 to 3, never falling along the last dimension, each value on 1 to 128 neighbouring positions
- w_query: bfloat16 [8, 8, 3072, 3072], P('rep', 'pipe', None, 'tp'), may hold values from -6 to 6
- w_key: bfloat16 [8, 8, 3072, 128], P('rep', 'pipe'), may hold values from -60 to 60
- gain: bfloat16 [8, 8, 3072], P('rep', 'pipe', 'tp'), may hold values from 0.5 to 1.5
- gossip_exp: int32 [8], P('pipe'), may hold values from 0 to 2
Outputs:
- next_input: bfloat16 [8, 8, 256, 3072], P('rep', 'pipe', None, 'tp')
- prev_grad: bfloat16 [8, 8, 256, 3072], P('rep', 'pipe', None, 'tp')
- w_query_out: bfloat16 [8, 8, 3072, 3072], P('rep', 'pipe', None, 'tp')
- w_key_out: bfloat16 [8, 8, 3072, 128], P('rep', 'pipe')
- gain_out: bfloat16 [8, 8, 3072], P('rep', 'pipe', 'tp')
Inputs may be any that keep to these rules, and one draw needn't show every extreme that they name: The partner of replica r at section p is r XOR 2^k with k = gossip_exp[p]. `seg_fwd`: along each section's rows the caption ids never fall; each caption has 1 to 128 tokens. `seg_bwd`: along each section's rows the caption ids never fall; each caption has 1 to 128 tokens.
All inputs are finite; a program needn't handle non-finite values.
Results may differ from a plain program's by a relative error of at most 0.015.
The roundings to bfloat16 on the way count: a program that leaves them out, or rounds other values in their place, can miss the bound.
Values may be sent and summed in bfloat16 or wider, within the bound.
A program may use at most 192 MiB of HBM per device.

v0:
```python
from functools import partial

import jax
import jax.numpy as jnp
from jax import lax
from jax.sharding import PartitionSpec as P

HEAD = 128


LN_EPS = 1e-05
STEP_EPS = 1e-06
LEARN_RATE = 0.2
MASK_FILL = -1e30


def shortened(shard):
    return jax.tree.map(lambda a: a.astype(jnp.bfloat16) if a.dtype == jnp.float32 else a, shard)


def swapped(block, axis, stride):
    count = lax.axis_size(axis)
    route = []
    for low in range(count):
        high = low | 1 << stride
        if high != low and high < count:
            route += [(low, high), (high, low)]
    return lax.ppermute(block, axis, route)


def from_behind(shard, axis, by):
    length = lax.axis_size(axis)
    return lax.ppermute(shard, axis, [(i, (i + by) % length) for i in range(length)])


def from_everyone(shard, axis):
    copies = jnp.broadcast_to(shard, (lax.axis_size(axis), *shard.shape))
    return lax.all_to_all(copies, axis, split_axis=0, concat_axis=0, tiled=True)


def of_everyone(shard, axis):
    return from_everyone(shard, axis).astype(jnp.float32).sum(axis=0)


def taken_together(shard, axis):
    everything = from_everyone(shard, axis)
    return jnp.sum(everything, axis=0)


def normalize(rows, gain_full):
    values = rows.astype(jnp.float32)
    centred = values - jnp.mean(values, axis=-1, keepdims=True)
    inv_std = lax.rsqrt(jnp.mean(centred * centred, axis=-1, keepdims=True) + LN_EPS)
    scaled = centred * inv_std
    normed = (scaled * gain_full.astype(jnp.float32)).astype(jnp.bfloat16)
    return (values, scaled, inv_std, normed)


def attend(normed, value_rows, caption, query_weight, key_weight):
    in_scale = normed.shape[1] ** (-0.5)
    count = normed.shape[0]
    heads = query_weight.shape[1] // HEAD
    queries = (jnp.dot(normed, query_weight, preferred_element_type=jnp.float32) * in_scale).astype(
        jnp.bfloat16
    )
    keys = (jnp.dot(normed, key_weight, preferred_element_type=jnp.float32) * in_scale).astype(
        jnp.bfloat16
    )
    query_heads = queries.reshape(count, heads, HEAD)
    value_heads = value_rows.reshape(count, heads, HEAD)
    scores = jnp.einsum(
        "rhd,sd->hrs", query_heads, keys, preferred_element_type=jnp.float32
    ) * HEAD ** (-0.5)
    same = caption[:, None] == caption[None, :]
    scores = jnp.where(same[None], scores, MASK_FILL)
    peak = jnp.max(scores, axis=-1, keepdims=True)
    expo = jnp.exp(scores - peak)
    probs = (expo / jnp.sum(expo, axis=-1, keepdims=True)).astype(jnp.bfloat16)
    mixed = jnp.einsum(
        "hrs,shd->rhd", probs, value_heads, preferred_element_type=jnp.float32
    ).reshape(count, -1)
    return (query_heads, keys, value_heads, probs, mixed)


def swap_updated(payload, bit):
    return jax.tree.map(
        lambda part, own: part.astype(own.dtype), swapped(shortened(payload), "rep", bit), payload
    )


def by_exponent(sender, exponent, payload):
    levels = lax.axis_size("rep").bit_length() - 1
    branches = [partial(sender, bit=level) for level in range(levels)]
    return lax.switch(exponent, branches, payload)


def updated(weight, step):
    return (weight.astype(jnp.float32) - step.astype(jnp.float32)).astype(jnp.bfloat16)


def halves(mine, theirs):
    return ((mine.astype(jnp.float32) + theirs.astype(jnp.float32)) * 0.5).astype(jnp.bfloat16)


def shards(fwd_in, bwd_in, bwd_grad, seg_fwd, seg_bwd, w_query, w_key, gain, gossip_exp):
    query_weight = w_query[0, 0]
    key_weight = w_key[0, 0]
    gain_local = gain[0, 0]
    fwd_rows = fwd_in[0, 0]
    bwd_rows = bwd_in[0, 0]
    grad_rows = bwd_grad[0, 0]
    local_width = fwd_rows.shape[1]
    count = fwd_rows.shape[0]
    tp_count = lax.axis_size("tp")
    pipe_count = lax.axis_size("pipe")
    offset = lax.axis_index("tp") * local_width
    exponent = gossip_exp[0]
    fwd_full, bwd_full, gain_full = (
        lax.all_gather(fwd_rows, "tp", axis=1, tiled=True),
        lax.all_gather(bwd_rows, "tp", axis=1, tiled=True),
        lax.all_gather(gain_local, "tp", axis=0, tiled=True),
    )
    width = fwd_full.shape[1]
    in_scale = width ** (-0.5)
    values, scaled, inv_std, normed = normalize(fwd_full, gain_full)
    own_values = lax.dynamic_slice_in_dim(normed, offset, local_width, 1)
    mixed = attend(normed, own_values, seg_fwd[0, 0], query_weight, key_weight)[4]
    section_out = (fwd_rows.astype(jnp.float32) + mixed).astype(jnp.bfloat16)
    next_rows = from_behind(section_out, "pipe", 1)
    values_b, scaled_b, inv_b, normed_b = normalize(bwd_full, gain_full)
    own_values_b = lax.dynamic_slice_in_dim(normed_b, offset, local_width, 1)
    query_heads, keys, value_heads, probs, unused = attend(
        normed_b, own_values_b, seg_bwd[0, 0], query_weight, key_weight
    )
    heads = local_width // HEAD
    grad_heads = grad_rows.reshape(count, heads, HEAD)
    value_grad = jnp.einsum(
        "hrs,rhd->shd", probs, grad_heads, preferred_element_type=jnp.float32
    ).reshape(count, local_width)
    prob_grad = jnp.einsum(
        "rhd,shd->hrs", grad_heads, value_heads, preferred_element_type=jnp.float32
    )
    prob_f = probs.astype(jnp.float32)
    score_grad = (
        prob_f * (prob_grad - jnp.sum(prob_grad * prob_f, axis=-1, keepdims=True)) * HEAD ** (-0.5)
    ).astype(jnp.bfloat16)
    query_grad = (
        jnp.einsum("hrs,sd->rhd", score_grad, keys, preferred_element_type=jnp.float32)
        .reshape(count, local_width)
        .astype(jnp.bfloat16)
    )
    key_part = jnp.einsum(
        "hrs,rhd->sd", score_grad, query_heads, preferred_element_type=jnp.float32
    )
    key_grad = (
        of_everyone(key_part.astype(jnp.bfloat16), "tp").astype(jnp.float32).astype(jnp.bfloat16)
    )
    contract_last = (((1,), (1,)), ((), ()))
    partial_grad = (
        lax.dot_general(query_grad, query_weight, contract_last, preferred_element_type=jnp.float32)
        * in_scale
    )
    own_cols = lax.dynamic_slice_in_dim(partial_grad, offset, local_width, 1) + value_grad
    partial_grad = lax.dynamic_update_slice_in_dim(partial_grad, own_cols, offset, 1)
    summed = of_everyone(partial_grad.astype(jnp.bfloat16), "tp").astype(jnp.float32)
    full_grad = (
        summed
        + lax.dot_general(key_grad, key_weight, contract_last, preferred_element_type=jnp.float32)
        * in_scale
    )
    weighted = full_grad * gain_full.astype(jnp.float32)
    full_input = inv_b * (
        weighted
        - jnp.mean(weighted, axis=-1, keepdims=True)
        - scaled_b * jnp.mean(weighted * scaled_b, axis=-1, keepdims=True)
    )
    input_grad = lax.dynamic_slice_in_dim(full_input, offset, local_width, 1)
    grad_gain = lax.dynamic_slice_in_dim(
        jnp.sum(full_grad * scaled_b, axis=0), offset, local_width, 0
    )
    back_rows = (grad_rows.astype(jnp.float32) + input_grad).astype(jnp.bfloat16)
    prev_rows = from_behind(back_rows, "pipe", -1)
    contract_first = (((0,), (0,)), ((), ()))
    grad_query = (
        lax.dot_general(normed_b, query_grad, contract_first, preferred_element_type=jnp.float32)
        * in_scale
    )
    grad_key = (
        lax.dot_general(normed_b, key_grad, contract_first, preferred_element_type=jnp.float32)
        * in_scale
    )
    local_squares = (
        jnp.sum(grad_query * grad_query)
        + jnp.sum(grad_gain * grad_gain)
        + jnp.sum(grad_key * grad_key) / tp_count
    )
    total_squares = taken_together(local_squares, ("pipe", "tp"))
    total = pipe_count * (width * width + width * HEAD + width)
    inverse = lax.rsqrt(total_squares / total + STEP_EPS)
    steps = (
        (LEARN_RATE * grad_query * inverse).astype(jnp.bfloat16),
        (LEARN_RATE * grad_key * inverse).astype(jnp.bfloat16),
        (LEARN_RATE * grad_gain * inverse).astype(jnp.bfloat16),
    )
    own_new = (
        updated(query_weight, steps[0]),
        updated(key_weight, steps[1]),
        updated(gain_local, steps[2]),
    )
    partner_new = by_exponent(swap_updated, exponent, own_new)
    query_out = halves(own_new[0], partner_new[0])
    key_out = halves(own_new[1], partner_new[1])
    gain_new = halves(own_new[2], partner_new[2])
    return (
        next_rows[None, None],
        prev_rows[None, None],
        query_out[None, None],
        key_out[None, None],
        gain_new[None, None],
    )


def solution(mesh):
    return jax.shard_map(
        shards,
        mesh=mesh,
        in_specs=(
            P("rep", "pipe", None, "tp"),
            P("rep", "pipe", None, "tp"),
            P("rep", "pipe", None, "tp"),
            P("rep", "pipe", None),
            P("rep", "pipe", None),
            P("rep", "pipe", None, "tp"),
            P("rep", "pipe", None, None),
            P("rep", "pipe", "tp"),
            P("pipe"),
        ),
        out_specs=(
            P("rep", "pipe", None, "tp"),
            P("rep", "pipe", None, "tp"),
            P("rep", "pipe", None, "tp"),
            P("rep", "pipe", None, None),
            P("rep", "pipe", "tp"),
        ),
        check_vma=False,
    )
```

profile of v0, /device:TPU:0, one launch (start us, length us, event | category | flops | bytes accessed | tf_op | source)
XLA Modules:
  0.0 470.2 jit_solution(6037535794319736713)
XLA Ops:
  9.4 6.1 %all-gather.1 = bf16[1,1,3072]{2,1,0:T(2,128)(2,1)S(1)} all-gather(bf16[1,1,1536]{2,1,0:T(2,128)(2,1)} %param.19), channel_id=3, replica_groups=mesh['rep'=8,'pipe'=8,'tp'=2] {'tp'}, dimensions={2}, use_global_device_ids=true | all-gather | bytes 9216 | tf_op jit(solution)/shard_map/all_gather | solution.py:121
  17.9 2.3 copy.66
  20.2 23.2 %all-gather.8.cloned.1.call-done = bf16[1,1,256,3072]{3,2,1,0:T(8,128)(2,1)} async-done(((bf16[1,1,256,1536]{3,2,1,0:T(8,128)(2,1)}), bf16[1,1,256,3072]{3,2,1,0:T(8,128)(2,1)}) %all-gather.8.cloned.1.call-update) | async-done | bytes 1572880 | tf_op jit(solution)/shard_map/all_gather | solution.py:120
  43.4 1.8 convert_reduce_fusion.1
  45.2 2.0 fusion.27
  49.4 2.3 copy.65
  51.7 7.7 %fusion.34 = bf16[256,1536]{1,0:T(8,128)(2,1)} fusion(bf16[256,3072]{1,0:T(8,128)(2,1)S(1)} %multiply_convert_fusion.1, bf16[1,1,3072,1536]{3,2,1,0:T(8,128)(2,1)} %param.17), kind=kOutput, calls=%fused_computation.50 | convolution fusion | flops 2416705536 | bytes 11796480 | tf_op jit(solution)/shard_map/dot_general | solution.py:63
  59.5 2.3 copy.63
  61.7 3.6 fusion.92
  65.4 3.9 fusion.90
  69.3 2.3 divide_convert_fusion
  72.7 1.8 fusion.93
  74.5 5.0 %fusion.65 = bf16[256,128]{1,0:T(8,128)(2,1)S(1)} fusion(bf16[256,12,128]{0,2,1:T(8,128)(2,1)} %bitcast.185, bf16[12,256,256]{1,2,0:T(8,128)(2,1)} %copy-done.11, f32[12,256,256]{2,1,0:T(8,128)} %fusion.92), kind=kOutput, calls=%fused_computation.88 | convolution fusion | flops 206867712 | bytes 5570560 | tf_op jit(solution)/shard_map/hrs,rhd->sd/dot_general | solution.py:152
  79.5 3.0 copy.72
  83.2 3.6 all-to-all-start.1
  86.8 5.7 %fusion.61 = bf16[128,12,256]{2,0,1:T(8,128)(2,1)} fusion(bf16[256,128,1]{1,0,2:T(8,128)(2,1)S(1)} %fusion.66, bf16[12,256,256]{1,2,0:T(8,128)(2,1)} %copy-done.11, f32[12,256,256]{2,1,0:T(8,128)} %fusion.92), kind=kOutput, calls=%fused_computation.82 | convolution fusion | flops 207228160 | bytes 5570560 | tf_op jit(solution)/shard_map/hrs,sd->rhd/dot_general | solution.py:148
  92.5 8.4 %fusion.13 = f32[256,3072]{1,0:T(8,128)} fusion(bf16[256,1536]{0,1:T(8,128)(2,1)} %bitcast.181, bf16[1,1,3072,1536]{3,2,1,0:T(8,128)(2,1)} %param.17), kind=kOutput, calls=%fused_computation.19 | convolution fusion | flops 2416705536 | bytes 13369344 | tf_op jit(solution)/shard_map/dot_general | solution.py:160
  100.9 2.8 add_dynamic-update-slice_fusion
  103.7 1.7 convert_reduce_fusion.2
  105.4 3.3 convert_element_type.185
  108.6 3.5 broadcast_in_dim.62
  112.1 5.2 %all-to-all-start = ((bf16[2,256,3072]{2,1,0:T(8,128)(2,1)}), bf16[2,256,3072]{2,1,0:T(8,128)(2,1)}, u32[]{:S(2)}, u32[]{:S(2)}) async-start(bf16[2,256,3072]{2,1,0:T(8,128)(2,1)} %broadcast_in_dim.62), calls=%async_computation | async-start | bytes 6291456 | tf_op jit(solution)/shard_map/all_to_all | solution.py:38
  117.3 2.0 fusion.21
  119.3 10.8 %multiply_reduce_fusion = (f32[]{:T(128)}, f32[3072,1536]{1,0:T(8,128)}) fusion(bf16[256,3072]{1,0:T(8,128)(2,1)S(1)} %multiply_convert_fusion.1, bf16[256,1536]{0,1:T(8,128)(2,1)} %bitcast.182), kind=kOutput, calls=%fused_computation.8 | convolution fusion | flops 2430074880 | bytes 21233668 | tf_op jit(solution)/shard_map/dot_general | solution.py:185
  130.1 2.6 multiply_reduce_fusion.3
  133.3 21.7 %all-to-all-done = bf16[2,256,3072]{2,1,0:T(8,128)(2,1)} async-done(((bf16[2,256,3072]{2,1,0:T(8,128)(2,1)}), bf16[2,256,3072]{2,1,0:T(8,128)(2,1)}, u32[]{:S(2)}, u32[]{:S(2)}) %all-to-all-start) | async-done | bytes 3145760 | tf_op jit(solution)/shard_map/all_to_all | solution.py:38
  155.1 2.9 convert_reduce_fusion
  158.0 3.6 fusion.89
  161.6 7.7 %fusion.37 = bf16[256,1536]{1,0:T(8,128)(2,1)} fusion(bf16[256,3072]{1,0:T(8,128)(2,1)S(1)} %get-tuple-element.70, bf16[1,1,3072,1536]{3,2,1,0:T(8,128)(2,1)} %param.17), kind=kOutput, calls=%fused_computation.51 | convolution fusion | flops 2416705536 | bytes 11796480 | tf_op jit(solution)/shard_map/dot_general | solution.py:63
  172.3 2.3 copy.58
  174.6 2.7 fusion.73
  177.3 4.1 fusion.91
  181.5 1.6 fusion.58
  183.1 1.9 copy.62
  185.0 2.2 fusion.49
  190.5 4.1 all-to-all-start.2
  194.6 2.3 fusion.48
  196.9 4.1 collective-permute-start.10
  201.0 6.9 %all-to-all-done.2 = f32[16,1,1]{2,1,0:T(1,128)S(1)} async-done(((f32[16,1,1]{2,1,0:T(1,128)}), f32[16,1,1]{2,1,0:T(1,128)S(1)}, u32[]{:S(2)}, u32[]{:S(2)}) %all-to-all-start.2) | async-done | bytes 96 | tf_op jit(solution)/shard_map/all_to_all | solution.py:38
  209.3 10.3 %subtract_convert_fusion = bf16[3072,1536]{1,0:T(8,128)(2,1)S(1)} fusion(f32[3072,1536]{1,0:T(8,128)} %get-tuple-element.76, bf16[1,1,3072,1536]{3,2,1,0:T(8,128)(2,1)} %param.17, f32[]{:T(128)S(6)} %mul.207), kind=kLoop, calls=%fused_computation.6 | loop fusion | flops 28311552 | bytes 37748740 | tf_op jit(solution)/shard_map/convert_element_type | solution.py:98
  220.0 3.4 copy-done
  223.4 221.3 %conditional.4 = (bf16[3072,1536]{1,0:T(8,128)(2,1)}, bf16[3072,128]{1,0:T(8,128)(2,1)}, bf16[1536]{0:T(1024)(128)(2,1)}) conditional(s32[]{:T(128)} %bitcast.30, (bf16[3072,1536]{1,0:T(8,128)(2,1)S(1)}, bf16[3072,128]{1,0:T(8,128)(2,1)S(1)}, bf16[1536]{0:T(1024)(128)(2,1)S(1)}) %tuple.46, (bf16[3072,1536]{1,0:T(8,128)(2,1)S(1)}, ...), branch_computations={%region_18.19_spmd, %region_19.20_spmd, %region_20.21_spmd} | conditional | bytes 40906896
  223.4 3.1 collective-permute-start.6
  226.9 3.1 collective-permute-start.8
  230.0 214.7 %collective-permute-done.8 = bf16[1536]{0:T(1024)(128)(2,1)} collective-permute-done((bf16[1536]{0:T(1024)(128)(2,1)S(1)}, bf16[1536]{0:T(1024)(128)(2,1)}, u32[]{:S(2)}, u32[]{:S(2)}) %collective-permute-start.8) | collective-permute-done | bytes 3104 | tf_op jit(solution)/shard_map/cond/branch_2_fun/ppermute | solution.py:28
  444.7 12.2 %fusion.5 = bf16[1,1,3072,1536]{3,2,1,0:T(8,128)(2,1)} fusion(bf16[3072,1536]{1,0:T(8,128)(2,1)} %get-tuple-element.62, bf16[3072,1536]{1,0:T(8,128)(2,1)} %copy-done), kind=kLoop, calls=%fused_computation.9 | loop fusion | flops 23592960 | bytes 28311552 | tf_op jit(solution)/shard_map/broadcast_in_dim | solution.py:217
  458.1 2.3 fusion.68
  460.4 2.1 copy.99
  (63 shorter events, 16.6 us)
Async XLA Ops:
  7.2 36.2 %all-gather.8.cloned.1.call-start = ((), (), s32[]{:S(2)}) async-start(), calls=%async_computation.4 | async-start | bytes 2359296 | tf_op jit(solution)/shard_map/all_gather | solution.py:120
  7.9 95.8 %all-gather.6.cloned.1.call-start = ((), (), s32[]{:S(2)}) async-start(), calls=%async_computation.3 | async-start | bytes 2359296 | tf_op jit(solution)/shard_map/all_gather | solution.py:119
  43.4 3.8 copy-start.1
  43.4 4.5 copy-start.3
  69.3 3.4 copy-start.8
  71.6 1.1 copy-start.11
  83.2 25.4 %all-to-all-start.1 = ((bf16[2,256,128]{2,1,0:T(8,128)(2,1)}), bf16[2,256,128]{2,1,0:T(8,128)(2,1)S(1)}, u32[]{:S(2)}, u32[]{:S(2)}) async-start(bf16[2,256,128]{2,1,0:T(8,128)(2,1)} %broadcast_in_dim.63), calls=%async_computation.1 | async-start | bytes 262144 | tf_op jit(solution)/shard_map/all_to_all | solution.py:38
  92.5 8.4 %copy-start.9 = (f32[256,1536]{1,0:T(8,128)S(1)}, f32[256,1536]{1,0:T(8,128)}, u32[]{:S(2)}) copy-start(f32[256,1536]{1,0:T(8,128)} %copy.72) | copy-start | bytes 4718596
  112.1 43.0 %all-to-all-start = ((bf16[2,256,3072]{2,1,0:T(8,128)(2,1)}), bf16[2,256,3072]{2,1,0:T(8,128)(2,1)}, u32[]{:S(2)}, u32[]{:S(2)}) async-start(bf16[2,256,3072]{2,1,0:T(8,128)(2,1)} %broadcast_in_dim.62), calls=%async_computation | async-start | bytes 6291456 | tf_op jit(solution)/shard_map/all_to_all | solution.py:38
  133.3 24.6 %copy-start.2 = (bf16[1,1,256,3072]{3,2,1,0:T(8,128)(2,1)S(1)}, bf16[1,1,256,3072]{3,2,1,0:T(8,128)(2,1)}, u32[]{:S(2)}) copy-start(bf16[1,1,256,3072]{3,2,1,0:T(8,128)(2,1)} %all-gather.6.cloned.1.call-done) | copy-start | bytes 4718596
  155.1 2.9 copy-start.4
  161.6 7.7 %copy-start.6 = (bf16[256,3072]{1,0:T(8,128)(2,1)}, bf16[256,3072]{1,0:T(8,128)(2,1)S(1)}, u32[]{:S(2)}) copy-start(bf16[256,3072]{1,0:T(8,128)(2,1)S(1)} %get-tuple-element.70) | copy-start | bytes 4718596
  169.3 5.3 %copy-start.5 = (bf16[1,1,3072,128]{3,2,1,0:T(8,128)(2,1)S(1)}, bf16[1,1,3072,128]{3,2,1,0:T(8,128)(2,1)}, u32[]{:S(2)}) copy-start(bf16[1,1,3072,128]{3,2,1,0:T(8,128)(2,1)} %param.18) | copy-start | bytes 2359300
  170.2 4.4 copy-start.7
  177.3 4.1 copy-start.13
  183.1 11.5 %copy-start.12 = (bf16[1,1,256,1536]{3,2,1,0:T(8,128)(2,1)S(1)}, bf16[1,1,256,1536]{3,2,1,0:T(8,128)(2,1)}, u32[]{:S(2)}) copy-start(bf16[1,1,256,1536]{3,2,1,0:T(8,128)(2,1)} %param.14) | copy-start | bytes 2359300
  187.2 273.2 %collective-permute-start.9 = (bf16[256,1536]{1,0:T(8,128)(2,1)}, bf16[256,1536]{1,0:T(8,128)(2,1)}, u32[]{:S(2)}, u32[]{:S(2)}) collective-permute-start(bf16[256,1536]{1,0:T(8,128)(2,1)} %fusion.49), channel_id=1, source_target_pairs={{0,2},{2,4},{4,6},{6,8},{8,10},{10,12},{12,14},{14,0},{1,3},{3,5},... | collective-permute-start | bytes 2359304 | tf_op jit(solution)/shard_map/ppermute | solution.py:33
  190.5 17.5 %all-to-all-start.2 = ((f32[16,1,1]{2,1,0:T(1,128)}), f32[16,1,1]{2,1,0:T(1,128)S(1)}, u32[]{:S(2)}, u32[]{:S(2)}) async-start(f32[16,1,1]{2,1,0:T(1,128)} %broadcast_in_dim.65), calls=%async_computation.2 | async-start | bytes 16384 | tf_op jit(solution)/shard_map/all_to_all | solution.py:38
  196.9 263.5 %collective-permute-start.10 = (bf16[256,1536]{1,0:T(8,128)(2,1)S(1)}, bf16[256,1536]{1,0:T(8,128)(2,1)S(1)}, u32[]{:S(2)}, u32[]{:S(2)}) collective-permute-start(bf16[256,1536]{1,0:T(8,128)(2,1)S(1)} %fusion.48), channel_id=1, source_target_pairs={{0,14},{2,0},{4,2},{6,4},{8,6},{10,8},{12,10},{14,12},{1,15},{3,1}... | collective-permute-start | bytes 2359304 | tf_op jit(solution)/shard_map/ppermute | solution.py:33
  209.3 10.4 %copy-start.10 = (f32[3072,128]{1,0:T(8,128)S(1)}, f32[3072,128]{1,0:T(8,128)}, u32[]{:S(2)}) copy-start(f32[3072,128]{1,0:T(8,128)} %get-tuple-element.78) | copy-start | bytes 4718596
  219.6 3.7 copy-start
  223.4 221.3 %collective-permute-start.6 = (bf16[3072,1536]{1,0:T(8,128)(2,1)S(1)}, bf16[3072,1536]{1,0:T(8,128)(2,1)}, u32[]{:S(2)}, u32[]{:S(2)}) collective-permute-start(bf16[3072,1536]{1,0:T(8,128)(2,1)S(1)} %get-tuple-element.42), channel_id=1, source_target_pairs={{0,64},{64,0},{16,80},{80,16},{32,96},{96,32},{48,112},{112,48},{1... | collective-permute-start | bytes 28311560 | tf_op jit(solution)/shard_map/cond/branch_2_fun/ppermute | solution.py:28
  226.4 218.3 %collective-permute-start.7 = (bf16[3072,128]{1,0:T(8,128)(2,1)S(1)}, bf16[3072,128]{1,0:T(8,128)(2,1)}, u32[]{:S(2)}, u32[]{:S(2)}) collective-permute-start(bf16[3072,128]{1,0:T(8,128)(2,1)S(1)} %get-tuple-element.43), channel_id=1, source_target_pairs={{0,64},{64,0},{16,80},{80,16},{32,96},{96,32},{48,112},{112,48},{1... | collective-permute-start | bytes 2359304 | tf_op jit(solution)/shard_map/cond/branch_2_fun/ppermute | solution.py:28
  226.9 217.8 %collective-permute-start.8 = (bf16[1536]{0:T(1024)(128)(2,1)S(1)}, bf16[1536]{0:T(1024)(128)(2,1)}, u32[]{:S(2)}, u32[]{:S(2)}) collective-permute-start(bf16[1536]{0:T(1024)(128)(2,1)S(1)} %get-tuple-element.44), channel_id=1, source_target_pairs={{0,64},{64,0},{16,80},{80,16},{32,96},{96,32},{48,112},{112,48},{1... | collective-permute-start | bytes 9224 | tf_op jit(solution)/shard_map/cond/branch_2_fun/ppermute | solution.py:28
Sparse Core Ops, SparseCore 0:
  9.6 33.7 all-gather.7
  45.0 30.6 all-gather.5
where the time goes:
time: 471 us; the launch traced here: 470 us
  waiting for transfers between devices  268 us (57%)
  matrix products  65.8 us (14%)
  other arithmetic  57.5 us (12%)
  local copies, waits for them, and re-layouts  30.3 us (6%)
  starting transfers between devices  25.1 us (5%)
  between operations  17.5 us (4%)
  blocking collectives  6.1 us (1%)
    ppermute x3, waiting for transfers between devices, swapped(): return lax.ppermute(block, axis, route)  215 us
    all_to_all x3, waiting for transfers between devices, from_everyone(): return lax.all_to_all(copies, axis, split_axis=0, concat_axis=0, tiled=True)  28.7 us
    all_gather x1, waiting for transfers between devices, shards(): lax.all_gather(bwd_rows, 'tp', axis=1, tiled=True)  23.2 us
    dot_general x2, matrix products, attend(): jnp.dot(normed, query_weight, preferred_element_type=jnp.float32) * in_scale  15.4 us
    all_to_all x3, starting transfers between devices, from_everyone(): return lax.all_to_all(copies, axis, split_axis=0, concat_axis=0, tiled=True)  12.9 us
    broadcast_in_dim x1, other arithmetic, shards(): query_out[None, None]  12.2 us
    dot_general x1, matrix products, shards(): lax.dot_general(normed_b, query_grad, contract_first, preferred_element_t...  10.8 us
    convert_element_type x3, other arithmetic, updated(): (weight.astype(jnp.float32) - step.astype(jnp.float32)).astype(jnp.bfloat16)  10.6 us
  transfers between devices with their start and end apart: 10, of which 4 were waited for; matrix products, arithmetic and copies ran while one was open for 23% of the time, Pallas kernels for 0%

commit v1 on v0

v1 whole, which is shorter than its diff:
```python
from functools import partial

import jax
import jax.numpy as jnp
from jax import lax
from jax.sharding import PartitionSpec as P

HEAD = 128


LN_EPS = 1e-05
STEP_EPS = 1e-06
LEARN_RATE = 0.2
MASK_FILL = -1e30
CHUNKS = 2


def from_behind(shard, axis, by):
    length = lax.axis_size(axis)
    return lax.ppermute(shard, axis, [(i, (i + by) % length) for i in range(length)])


def flipped(block, axis, bit):
    return lax.ppermute(block, axis, [(i, i ^ 1 << bit) for i in range(lax.axis_size(axis))])


def in_order(own, other, low, axis):
    return jnp.where(
        low, jnp.concatenate([own, other], axis), jnp.concatenate([other, own], axis)
    )


def of_everyone(shard, axis):
    copies = jnp.broadcast_to(shard, (lax.axis_size(axis), *shard.shape))
    return jnp.sum(lax.all_to_all(copies, axis, split_axis=0, concat_axis=0, tiled=True), axis=0)


class Gossip:
    def __init__(self, exponent):
        self.exponent = exponent
        self.odd = (lax.axis_index("rep") // 2) % 2
        self.one = exponent == 1

    def first(self, up, down):
        return from_behind(up, "rep", 2), from_behind(down, "rep", -2), up, down

    def second(self, state):
        above, below, up, down = state
        return (
            from_behind(jnp.where(self.one, down, above), "rep", 2),
            from_behind(jnp.where(self.one, up, below), "rep", -2),
        )

    def case(self):
        return jnp.where(self.exponent == 2, 3, jnp.where(self.one, 1 + self.odd, 0))

    def choices(self, near, state, later):
        above, below = state[:2]
        from_up, from_down = later
        return (near, (from_down, below), (above, from_up), (from_up, from_down))

    def pick(self, near, state, later):
        sets = self.choices(near, state, later)
        case = self.case()
        return [
            jnp.where(case == 0, a, jnp.where(case == 1, b, jnp.where(case == 2, c, d)))
            for a, b, c, d in zip(*sets)
        ]

    def small(self, block):
        half = block.shape[0] // 2
        up, down = block[:half], block[half:]
        state = self.first(up, down)
        later = self.second(state)
        near = flipped(block, "rep", 0)
        return jnp.concatenate(self.pick((near[:half], near[half:]), state, later), axis=0)

    def tiny(self, block):
        results = [flipped(block, "rep", bit) for bit in range(3)]
        return jnp.where(
            self.exponent == 0, results[0], jnp.where(self.one, results[1], results[2])
        )


def normalize(rows, gain_full):
    values = rows.astype(jnp.float32)
    centred = values - jnp.mean(values, axis=-1, keepdims=True)
    inv_std = lax.rsqrt(jnp.mean(centred * centred, axis=-1, keepdims=True) + LN_EPS)
    scaled = centred * inv_std
    normed = (scaled * gain_full.astype(jnp.float32)).astype(jnp.bfloat16)
    return (values, scaled, inv_std, normed)


def attend(normed, value_rows, caption, query_weight, key_weight):
    in_scale = normed.shape[1] ** (-0.5)
    count = normed.shape[0]
    heads = query_weight.shape[1] // HEAD
    queries = (jnp.dot(normed, query_weight, preferred_element_type=jnp.float32) * in_scale).astype(
        jnp.bfloat16
    )
    keys = (jnp.dot(normed, key_weight, preferred_element_type=jnp.float32) * in_scale).astype(
        jnp.bfloat16
    )
    query_heads = queries.reshape(count, heads, HEAD)
    value_heads = value_rows.reshape(count, heads, HEAD)
    scores = jnp.einsum(
        "rhd,sd->hrs", query_heads, keys, preferred_element_type=jnp.float32
    ) * HEAD ** (-0.5)
    same = caption[:, None] == caption[None, :]
    scores = jnp.where(same[None], scores, MASK_FILL)
    peak = jnp.max(scores, axis=-1, keepdims=True)
    expo = jnp.exp(scores - peak)
    probs = (expo / jnp.sum(expo, axis=-1, keepdims=True)).astype(jnp.bfloat16)
    return (query_heads, keys, value_heads, probs)


def updated(weight, step):
    return (weight.astype(jnp.float32) - step.astype(jnp.float32)).astype(jnp.bfloat16)


def halves(mine, theirs):
    return ((mine.astype(jnp.float32) + theirs.astype(jnp.float32)) * 0.5).astype(jnp.bfloat16)


def shards(fwd_in, bwd_in, bwd_grad, seg_fwd, seg_bwd, w_query, w_key, gain, gossip_exp):
    query_weight = w_query[0, 0]
    key_weight = w_key[0, 0]
    gain_local = gain[0, 0]
    fwd_rows = fwd_in[0, 0]
    bwd_rows = bwd_in[0, 0]
    grad_rows = bwd_grad[0, 0]
    count, local_width = fwd_rows.shape
    tp_count = lax.axis_size("tp")
    pipe_count = lax.axis_size("pipe")
    tp_index = lax.axis_index("tp")
    low = tp_index == 0
    offset = tp_index * local_width
    gossip = Gossip(gossip_exp[0])

    bwd_full = in_order(bwd_rows, flipped(bwd_rows, "tp", 0), low, 1)
    gain_full = in_order(gain_local, flipped(gain_local, "tp", 0), low, 0)
    width = bwd_full.shape[1]
    in_scale = width ** (-0.5)

    step_rows = width // (2 * CHUNKS)
    parts = [query_weight[i * step_rows : (i + 1) * step_rows] for i in range(2 * CHUNKS)]
    sent = [gossip.first(parts[i], parts[CHUNKS + i]) for i in range(CHUNKS)]
    query_near = flipped(query_weight, "rep", 0)

    values_b, scaled_b, inv_b, normed_b = normalize(bwd_full, gain_full)
    own_values_b = lax.dynamic_slice_in_dim(normed_b, offset, local_width, 1)
    normed_half = gossip.small(own_values_b)
    normed_partner = in_order(normed_half, flipped(normed_half, "tp", 0), low, 1)
    key_half = gossip.small(lax.dynamic_slice_in_dim(key_weight, offset, local_width, 0))
    key_partner = in_order(key_half, flipped(key_half, "tp", 0), low, 0)

    query_heads, keys, value_heads, probs = attend(
        normed_b, own_values_b, seg_bwd[0, 0], query_weight, key_weight
    )
    heads = local_width // HEAD
    grad_heads = grad_rows.reshape(count, heads, HEAD)
    prob_grad = jnp.einsum(
        "rhd,shd->hrs", grad_heads, value_heads, preferred_element_type=jnp.float32
    )
    prob_f = probs.astype(jnp.float32)
    score_grad = (
        prob_f * (prob_grad - jnp.sum(prob_grad * prob_f, axis=-1, keepdims=True)) * HEAD ** (-0.5)
    ).astype(jnp.bfloat16)
    query_grad = (
        jnp.einsum("hrs,sd->rhd", score_grad, keys, preferred_element_type=jnp.float32)
        .reshape(count, local_width)
        .astype(jnp.bfloat16)
    )
    query_grad_partner = gossip.small(query_grad)
    key_part = jnp.einsum(
        "hrs,rhd->sd", score_grad, query_heads, preferred_element_type=jnp.float32
    ).astype(jnp.bfloat16)
    key_grad = (
        key_part.astype(jnp.float32) + flipped(key_part, "tp", 0).astype(jnp.float32)
    ).astype(jnp.bfloat16)
    key_grad_partner = gossip.small(key_grad)
    value_grad = jnp.einsum(
        "hrs,rhd->shd", probs, grad_heads, preferred_element_type=jnp.float32
    ).reshape(count, local_width)

    contract_last = (((1,), (1,)), ((), ()))
    partial_grad = (
        lax.dot_general(query_grad, query_weight, contract_last, preferred_element_type=jnp.float32)
        * in_scale
    )
    own_part = (lax.dynamic_slice_in_dim(partial_grad, offset, local_width, 1) + value_grad).astype(
        jnp.bfloat16
    )
    other_part = lax.dynamic_slice_in_dim(
        partial_grad, local_width - offset, local_width, 1
    ).astype(jnp.bfloat16)
    from_other = flipped(other_part, "tp", 0)
    key_rows = lax.dynamic_slice_in_dim(key_weight, offset, local_width, 0)
    full_grad = (
        own_part.astype(jnp.float32)
        + from_other.astype(jnp.float32)
        + lax.dot_general(key_grad, key_rows, contract_last, preferred_element_type=jnp.float32)
        * in_scale
    )
    own_scaled = lax.dynamic_slice_in_dim(scaled_b, offset, local_width, 1)
    weighted = full_grad * gain_local.astype(jnp.float32)
    sums = jnp.stack([jnp.sum(weighted, axis=-1), jnp.sum(weighted * own_scaled, axis=-1)])
    means = (sums + flipped(sums, "tp", 0)) / width
    input_grad = inv_b * (weighted - means[0][:, None] - own_scaled * means[1][:, None])
    grad_gain = jnp.sum(full_grad * own_scaled, axis=0)
    back_rows = (grad_rows.astype(jnp.float32) + input_grad).astype(jnp.bfloat16)
    prev_rows = from_behind(back_rows, "pipe", -1)

    fwd_full = in_order(fwd_rows, flipped(fwd_rows, "tp", 0), low, 1)
    values, scaled, inv_std, normed = normalize(fwd_full, gain_full)
    own_values = lax.dynamic_slice_in_dim(normed, offset, local_width, 1)
    unused_q, unused_k, value_heads_f, probs_f = attend(
        normed, own_values, seg_fwd[0, 0], query_weight, key_weight
    )
    mixed = jnp.einsum(
        "hrs,shd->rhd", probs_f, value_heads_f, preferred_element_type=jnp.float32
    ).reshape(count, -1)
    section_out = (fwd_rows.astype(jnp.float32) + mixed).astype(jnp.bfloat16)
    next_rows = from_behind(section_out, "pipe", 1)

    contract_first = (((0,), (0,)), ((), ()))

    def weight_grad(rows, grad):
        return (
            lax.dot_general(rows, grad, contract_first, preferred_element_type=jnp.float32)
            * in_scale
        )

    grad_query = weight_grad(normed_b, query_grad)
    grad_key = weight_grad(normed_b, key_grad)
    local_squares = (
        jnp.sum(grad_query * grad_query)
        + jnp.sum(grad_gain * grad_gain)
        + jnp.sum(grad_key * grad_key) / tp_count
    )
    total_squares = of_everyone(local_squares, ("pipe", "tp"))
    total = pipe_count * (width * width + width * HEAD + width)
    inverse = lax.rsqrt(total_squares / total + STEP_EPS)

    def step_of(gradient, scale):
        return (LEARN_RATE * gradient * scale).astype(jnp.bfloat16)

    gain_new = updated(gain_local, step_of(grad_gain, inverse))
    both = gossip.tiny(
        jnp.concatenate(
            [gain_new.astype(jnp.float32), jnp.broadcast_to(inverse, (HEAD,))]
        )
    )
    gain_partner = both[:local_width].astype(jnp.bfloat16)
    inverse_partner = both[local_width]
    gain_out = halves(gain_new, gain_partner)

    key_out = halves(
        updated(key_weight, step_of(grad_key, inverse)),
        updated(
            key_partner,
            step_of(weight_grad(normed_partner, key_grad_partner), inverse_partner),
        ),
    )
    query_new = updated(query_weight, step_of(grad_query, inverse))
    query_step_partner = step_of(weight_grad(normed_partner, query_grad_partner), inverse_partner)

    later = [gossip.second(state) for state in sent]
    ups, downs = zip(*later)
    nears = [query_near[i * step_rows : (i + 1) * step_rows] for i in range(2 * CHUNKS)]
    candidates = [
        gossip.choices((nears[i], nears[CHUNKS + i]), sent[i], later[i]) for i in range(CHUNKS)
    ]

    def averaged(case, candidates, new, step):
        picked = [c[case] for c in candidates]
        weight = jnp.concatenate([p[0] for p in picked] + [p[1] for p in picked], axis=0)
        return halves(new, updated(weight, step))

    query_out = lax.switch(
        gossip.case(),
        [partial(averaged, case) for case in range(4)],
        candidates,
        query_new,
        query_step_partner,
    )
    return (
        next_rows[None, None],
        prev_rows[None, None],
        query_out[None, None],
        key_out[None, None],
        gain_out[None, None],
    )


def solution(mesh):
    return jax.shard_map(
        shards,
        mesh=mesh,
        in_specs=(
            P("rep", "pipe", None, "tp"),
            P("rep", "pipe", None, "tp"),
            P("rep", "pipe", None, "tp"),
            P("rep", "pipe", None),
            P("rep", "pipe", None),
            P("rep", "pipe", None, "tp"),
            P("rep", "pipe", None, None),
            P("rep", "pipe", "tp"),
            P("pipe"),
        ),
        out_specs=(
            P("rep", "pipe", None, "tp"),
            P("rep", "pipe", None, "tp"),
            P("rep", "pipe", None, "tp"),
            P("rep", "pipe", None, None),
            P("rep", "pipe", "tp"),
        ),
        check_vma=False,
    )
```

time: 471 us -> 477 us (1.013)
  the two profiles are of different devices: /device:TPU:0 before, /device:TPU:24 now
where the time goes in v1:
time: 477 us; the launch traced here: 470 us
  waiting for transfers between devices  206 us (43%)
  other arithmetic  78.4 us (16%)
  matrix products  71.2 us (15%)
  starting transfers between devices  62.2 us (13%)
  local copies, waits for them, and re-layouts  46.2 us (10%)
  between operations  5.65 us (1%)
    ppermute x26, waiting for transfers between devices, from_behind(): lax.ppermute(shard, axis, [(i, (i + by) % length) for i in range(length)])  184 us
    ppermute x26, starting transfers between devices, from_behind(): lax.ppermute(shard, axis, [(i, (i + by) % length) for i in range(length)])  36.9 us
    dot_general x4, matrix products, weight_grad(): lax.dot_general(rows, grad, contract_first, preferred_element_type=jnp.fl...  22.6 us
    ppermute x16, waiting for transfers between devices, flipped(): lax.ppermute(block, axis, [(i, i ^ 1 << bit) for i in range(lax.axis_size...  22.1 us
    ppermute x16, starting transfers between devices, flipped(): lax.ppermute(block, axis, [(i, i ^ 1 << bit) for i in range(lax.axis_size...  18.1 us
    select_n x5, other arithmetic, second(): jnp.where(self.one, down, above)  16.1 us
    broadcast_in_dim x1, other arithmetic, shards(): query_out[None, None]  11 us
  transfers between devices with their start and end apart: 43, of which 12 were waited for; matrix products, arithmetic and copies ran while one was open for 38% of the time, Pallas kernels for 0%

profile of v1, /device:TPU:24, one launch (start us, length us, event | category | flops | bytes accessed | tf_op | source)
XLA Modules:
  0.0 469.9 jit_solution(10118504313165606883)
XLA Ops:
  3.8 4.1 collective-permute-start.32
  15.8 3.2 collective-permute-start.33
  19.0 3.5 collective-permute-done.34
  28.2 3.7 collective-permute-done.35
  35.9 12.9 %collective-permute-done = bf16[256,1536]{1,0:T(8,128)(2,1)S(1)} collective-permute-done((bf16[256,1536]{1,0:T(8,128)(2,1)S(1)}, bf16[256,1536]{1,0:T(8,128)(2,1)S(1)}, u32[]{:S(2)}, u32[]{:S(2)}) %collective-permute-start) | collective-permute-done | bytes 786464 | tf_op jit(solution)/shard_map/ppermute | solution.py:24
  49.9 5.0 %multiply_convert_fusion.6 = (bf16[256,3072]{1,0:T(8,128)(2,1)S(1)}, f32[256,3072]{1,0:T(8,128)}, bf16[256,3072]{1,0:T(8,128)(2,1)S(1)}) fusion(f32[3072]{0:T(1024)S(1)} %fusion.58, f32[256]{0:T(256)S(1)} %add_rsqrt_fusion, f32[256]{0:T(256)S(1)} %broadcast_multiply_fusion, bf16[256,1536]{1,0:T(8,128)(2,1)S(1)} %bitcast.189, ...), kind=kLoop, calls=%fused_computation.44 | loop fusion | flops 22020096 | bytes 9453569 | tf_op jit(solution)/shard_map/convert_element_type | solution.py:90
  57.4 3.5 fusion.19
  60.9 3.5 fusion.20
  66.6 2.3 copy.75
  69.0 3.6 fusion.79
  72.6 3.9 fusion.78
  76.5 3.4 divide_convert_fusion
  79.9 5.8 %fusion.40 = bf16[256,128]{1,0:T(8,128)(2,1)} fusion(bf16[256,12,128]{0,2,1:T(8,128)(2,1)} %bitcast.201, bf16[12,256,256]{1,2,0:T(8,128)(2,1)} %divide_convert_fusion, f32[12,256,256]{2,1,0:T(8,128)} %fusion.79), kind=kOutput, calls=%fused_computation.97 | convolution fusion | flops 206867712 | bytes 5570560 | tf_op jit(solution)/shard_map/hrs,rhd->sd/dot_general | solution.py:175
  85.7 5.9 %fusion.36 = bf16[128,12,256]{2,0,1:T(8,128)(2,1)} fusion(bf16[256,128,1]{1,0,2:T(8,128)(2,1)S(1)} %fusion.41, bf16[12,256,256]{1,2,0:T(8,128)(2,1)} %divide_convert_fusion, f32[12,256,256]{2,1,0:T(8,128)} %fusion.79), kind=kOutput, calls=%fused_computation.90 | convolution fusion | flops 207228160 | bytes 5570560 | tf_op jit(solution)/shard_map/hrs,sd->rhd/dot_general | solution.py:170
  91.6 3.5 fusion.80
  95.0 8.0 %convolution_multiply_fusion = f32[256,3072]{1,0:T(8,128)} fusion(bf16[256,1536]{0,1:T(8,128)(2,1)S(1)} %bitcast.182, bf16[1,1,3072,1536]{3,2,1,0:T(8,128)(2,1)} %param.18), kind=kOutput, calls=%fused_computation.19 | convolution fusion | flops 2416705536 | bytes 13369344 | tf_op jit(solution)/shard_map/dot_general | solution.py:188
  103.1 10.0 %multiply_reduce_fusion = (f32[]{:T(128)}, f32[3072,1536]{1,0:T(8,128)}) fusion(bf16[256,3072]{1,0:T(8,128)(2,1)S(1)} %get-tuple-element.88, bf16[256,1536]{0,1:T(8,128)(2,1)S(1)} %bitcast.183), kind=kOutput, calls=%fused_computation.18 | convolution fusion | flops 2430074880 | bytes 21233668 | tf_op jit(solution)/shard_map/dot_general | solution.py:230
  113.9 3.2 collective-permute-start.10
  121.7 4.4 fusion.50
  126.0 4.2 fusion.77
  131.8 3.1 copy.74
  134.9 2.5 add_convert_fusion.1
  139.8 3.1 copy.84
  152.2 2.4 dynamic-slice_convert_fusion
  158.4 3.4 multiply_reduce_fusion.1
  173.6 7.6 %collective-permute-done.4 = bf16[256,1536]{1,0:T(8,128)(2,1)S(1)} collective-permute-done((bf16[256,1536]{1,0:T(8,128)(2,1)}, bf16[256,1536]{1,0:T(8,128)(2,1)S(1)}, u32[]{:S(2)}, u32[]{:S(2)}) %collective-permute-start.4) | collective-permute-done | bytes 786464 | tf_op jit(solution)/shard_map/ppermute | solution.py:24
  181.5 4.5 multiply_reduce_fusion.2
  188.6 7.1 %all-to-all-start = ((f32[16,1,1]{2,1,0:T(1,128)}), f32[16,1,1]{2,1,0:T(1,128)}, u32[]{:S(2)}, u32[]{:S(2)}) async-start(f32[16,1,1]{2,1,0:T(1,128)} %broadcast_in_dim.66), calls=%async_computation | async-start | bytes 16384 | tf_op jit(solution)/shard_map/all_to_all | solution.py:35
  197.9 3.2 collective-permute-start.17
  206.6 12.1 %collective-permute-done.2 = bf16[256,1536]{1,0:T(8,128)(2,1)S(1)} collective-permute-done((bf16[256,1536]{1,0:T(8,128)(2,1)}, bf16[256,1536]{1,0:T(8,128)(2,1)S(1)}, u32[]{:S(2)}, u32[]{:S(2)}) %collective-permute-start.2) | collective-permute-done | bytes 786464 | tf_op jit(solution)/shard_map/ppermute | solution.py:20
  221.5 3.5 collective-permute-start.22
  224.9 6.9 %slice_bitcast_fusion.1 = (bf16[768,1536]{1,0:T(8,128)(2,1)}, bf16[768,1536]{1,0:T(8,128)(2,1)}, bf16[768,1536]{1,0:T(8,128)(2,1)}, bf16[768,1536]{1,0:T(8,128)(2,1)}) fusion(bf16[1,1,3072,1536]{3,2,1,0:T(8,128)(2,1)} %param.18), kind=kLoop, calls=%fused_computation.55 | loop fusion | bytes 18874368 | tf_op jit(solution)/shard_map/slice | solution.py:146
  231.9 3.2 collective-permute-start.23
  235.1 3.2 collective-permute-start.25
  239.8 2.4 slice_select_fusion.1
  247.5 40.0 %collective-permute-done.28 = bf16[768,1536]{1,0:T(8,128)(2,1)} collective-permute-done((bf16[768,1536]{1,0:T(8,128)(2,1)}, bf16[768,1536]{1,0:T(8,128)(2,1)}, u32[]{:S(2)}, u32[]{:S(2)}) %collective-permute-start.28) | collective-permute-done | bytes 2359328 | tf_op jit(solution)/shard_map/ppermute | solution.py:20
  287.5 49.3 %collective-permute-done.27 = bf16[768,1536]{1,0:T(8,128)(2,1)} collective-permute-done((bf16[768,1536]{1,0:T(8,128)(2,1)}, bf16[768,1536]{1,0:T(8,128)(2,1)}, u32[]{:S(2)}, u32[]{:S(2)}) %collective-permute-start.27) | collective-permute-done | bytes 2359328 | tf_op jit(solution)/shard_map/ppermute | solution.py:20
  336.8 3.5 collective-permute-start.14
  340.3 10.4 %broadcast_select_fusion = (bf16[768,1536]{1,0:T(8,128)(2,1)}, bf16[768,1536]{1,0:T(8,128)(2,1)}, bf16[768,1536]{1,0:T(8,128)(2,1)}, bf16[768,1536]{1,0:T(8,128)(2,1)}) fusion(bf16[768,1536]{1,0:T(8,128)(2,1)} %collective-permute-done.28, pred[]{:T(512)} %bitcast.37, bf16[1,1,3072,1536]{3,2,1,0:T(8,128)(2,1)} %param.18, ...), kind=kLoop, calls=%fused_computation.58 | loop fusion | flops 4718592 | bytes 28311552 | tf_op jit(solution)/shard_map/jit(_where)/select_n | solution.py:50
  350.9 3.2 collective-permute-start.26
  356.6 2.9 collective-permute-start.24
  359.5 8.4 %subtract_convert_fusion.4 = bf16[3072,1536]{1,0:T(8,128)(2,1)S(1)} fusion(f32[3072,1536]{1,0:T(8,128)} %get-tuple-element.119, f32[]{:T(128)S(6)} %mul.236, bf16[1,1,3072,1536]{3,2,1,0:T(8,128)(2,1)S(1)} %bitcast.177), kind=kLoop, calls=%fused_computation.16 | loop fusion | flops 28311552 | bytes 37748740 | tf_op jit(solution)/shard_map/convert_element_type | solution.py:118
  370.6 4.5 multiply_convert_fusion.4
  375.1 4.8 %fusion.43 = bf16[1,1,3072,128]{3,2,1,0:T(8,128)(2,1)} fusion(f32[3072,128]{1,0:T(8,128)} %get-tuple-element.121, bf16[1536,128]{1,0:T(8,128)(2,1)} %collective-permute-done.36, bf16[768,128]{1,0:T(8,128)(2,1)} %copy-done.26, bf16[768,128]{1,0:T(8,128)(2,1)} %copy-done.25, bf16[1,1,3072,128]{3,2,1,0:T(8,128)(2,1)} %param.19, f32[]{:T(128)} %bitcast.42, ...), kind=kOutput, calls=%fused_computation.100 | convolution fusion | flops 223477760 | bytes 5570569 | tf_op jit(solution)/shard_map/dot_general | solution.py:230
  379.8 26.7 %collective-permute-done.30 = bf16[768,1536]{1,0:T(8,128)(2,1)} collective-permute-done((bf16[768,1536]{1,0:T(8,128)(2,1)}, bf16[768,1536]{1,0:T(8,128)(2,1)}, u32[]{:S(2)}, u32[]{:S(2)}) %collective-permute-start.30) | collective-permute-done | bytes 2359328 | tf_op jit(solution)/shard_map/ppermute | solution.py:20
  406.5 47.9 %collective-permute-done.29 = bf16[768,1536]{1,0:T(8,128)(2,1)} collective-permute-done((bf16[768,1536]{1,0:T(8,128)(2,1)}, bf16[768,1536]{1,0:T(8,128)(2,1)}, u32[]{:S(2)}, u32[]{:S(2)}) %collective-permute-start.29) | collective-permute-done | bytes 2359328 | tf_op jit(solution)/shard_map/ppermute | solution.py:20
  454.4 11.0 %conditional.1 = (bf16[1,1,3072,1536]{3,2,1,0:T(8,128)(2,1)}) conditional(s32[]{:T(128)} %clamp.3, (bf16[3072,1536]{1,0:T(8,128)(2,1)S(1)}, bf16[3072,1536]{1,0:T(8,128)(2,1)}, bf16[3072,1536]{1,0:T(8,128)(2,1)S(1)}) %tuple.24, (bf16[3072,1536]{1,0:T(8,128)(2,1)S(1)}, bf16[768,1536]{1,0:T(8,128)(2,1)}, ...), branch_computations={%region_16.17_spmd, %region_17.18_spmd, %region_18.19_spmd, %regio... | conditional | flops 75497472 | bytes 37748744 | solution.py:280
  454.4 11.0 %fusion = bf16[1,1,3072,1536]{3,2,1,0:T(8,128)(2,1)} fusion(bf16[3072,1536]{1,0:T(8,128)(2,1)S(1)} %get-tuple-element.57, bf16[3072,1536]{1,0:T(8,128)(2,1)} %get-tuple-element.56, bf16[3072,1536]{1,0:T(8,128)(2,1)S(1)} %get-tuple-element.55), kind=kLoop, calls=%fused_computation.2 | loop fusion | flops 42467328 | bytes 37748736 | tf_op jit(solution)/shard_map/broadcast_in_dim | solution.py:290
  (214 shorter events, 86.0 us)
Async XLA Ops:
  1.5 32.7 %copy-start.30 = (bf16[1536]{0:T(1024)(128)(2,1)}, bf16[1536]{0:T(1024)(128)(2,1)S(1)}, u32[]{:S(2)}) copy-start(bf16[1536]{0:T(1024)(128)(2,1)S(1)} %reduce.1) | copy-start | bytes 9220
  1.5 25.4 %collective-permute-start.1 = (bf16[1536]{0:T(1024)(128)(2,1)S(1)}, bf16[1536]{0:T(1024)(128)(2,1)S(1)}, u32[]{:S(2)}, u32[]{:S(2)}) collective-permute-start(bf16[1536]{0:T(1024)(128)(2,1)S(1)} %reduce.1), channel_id=1, source_target_pairs={{0,1},{1,0},{2,3},{3,2},{4,5},{5,4},{6,7},{7,6},{8,9},{9,8},{10,11... | collective-permute-start | bytes 9224 | tf_op jit(solution)/shard_map/ppermute | solution.py:24
  3.8 31.1 %copy-start.8 = (bf16[1,1,256,1536]{3,2,1,0:T(8,128)(2,1)S(1)}, bf16[1,1,256,1536]{3,2,1,0:T(8,128)(2,1)}, u32[]{:S(2)}) copy-start(bf16[1,1,256,1536]{3,2,1,0:T(8,128)(2,1)} %param.14) | copy-start | bytes 2359300
  3.8 8.8 %collective-permute-start.32 = (bf16[768,128]{1,0:T(8,128)(2,1)S(1)}, bf16[768,128]{1,0:T(8,128)(2,1)S(1)}, u32[]{:S(2)}, u32[]{:S(2)}) collective-permute-start(bf16[768,128]{1,0:T(8,128)(2,1)S(1)} %dynamic-slice_bitcast_fusion.1), channel_id=1, source_target_pairs={{0,96},{16,112},{32,0},{48,16},{64,32},{80,48},{96,64},{112,80},{1... | collective-permute-start | bytes 589832 | tf_op jit(solution)/shard_map/ppermute | solution.py:20
  9.6 18.5 %collective-permute-start.31 = (bf16[1536,128]{1,0:T(8,128)(2,1)}, bf16[1536,128]{1,0:T(8,128)(2,1)}, u32[]{:S(2)}, u32[]{:S(2)}) collective-permute-start(bf16[1536,128]{1,0:T(8,128)(2,1)} %dynamic-slice_bitcast_fusion), channel_id=1, source_target_pairs={{0,16},{16,0},{32,48},{48,32},{64,80},{80,64},{96,112},{112,96},{1... | collective-permute-start | bytes 1179656 | tf_op jit(solution)/shard_map/ppermute | solution.py:24
  9.6 25.2 %collective-permute-start.3 = (bf16[256,1536]{1,0:T(8,128)(2,1)}, bf16[256,1536]{1,0:T(8,128)(2,1)S(1)}, u32[]{:S(2)}, u32[]{:S(2)}) collective-permute-start(bf16[256,1536]{1,0:T(8,128)(2,1)} %bitcast.186), channel_id=1, source_target_pairs={{0,1},{1,0},{2,3},{3,2},{4,5},{5,4},{6,7},{7,6},{8,9},{9,8},{10,11... | collective-permute-start | bytes 2359304 | tf_op jit(solution)/shard_map/ppermute | solution.py:24
  14.3 8.2 %collective-permute-start.34 = (bf16[768,128]{1,0:T(8,128)(2,1)S(1)}, bf16[768,128]{1,0:T(8,128)(2,1)S(1)}, u32[]{:S(2)}, u32[]{:S(2)}) collective-permute-start(bf16[768,128]{1,0:T(8,128)(2,1)S(1)} %get-tuple-element.85), channel_id=1, source_target_pairs={{0,32},{16,48},{32,64},{48,80},{64,96},{80,112},{96,0},{112,16},{1... | collective-permute-start | bytes 589832 | tf_op jit(solution)/shard_map/ppermute | solution.py:20
  15.8 12.4 %collective-permute-start.33 = (bf16[768,128]{1,0:T(8,128)(2,1)}, bf16[768,128]{1,0:T(8,128)(2,1)}, u32[]{:S(2)}, u32[]{:S(2)}) collective-permute-start(bf16[768,128]{1,0:T(8,128)(2,1)} %get-tuple-element.84), channel_id=1, source_target_pairs={{0,96},{16,112},{32,0},{48,16},{64,32},{80,48},{96,64},{112,80},{1... | collective-permute-start | bytes 589832 | tf_op jit(solution)/shard_map/ppermute | solution.py:20
  24.2 7.7 %collective-permute-start.35 = (bf16[768,128]{1,0:T(8,128)(2,1)}, bf16[768,128]{1,0:T(8,128)(2,1)}, u32[]{:S(2)}, u32[]{:S(2)}) collective-permute-start(bf16[768,128]{1,0:T(8,128)(2,1)} %broadcast_select_fusion.8), channel_id=1, source_target_pairs={{0,32},{16,48},{32,64},{48,80},{64,96},{80,112},{96,0},{112,16},{1... | collective-permute-start | bytes 589832 | tf_op jit(solution)/shard_map/ppermute | solution.py:20
  26.9 21.9 %collective-permute-start = (bf16[256,1536]{1,0:T(8,128)(2,1)S(1)}, bf16[256,1536]{1,0:T(8,128)(2,1)S(1)}, u32[]{:S(2)}, u32[]{:S(2)}) collective-permute-start(bf16[256,1536]{1,0:T(8,128)(2,1)S(1)} %bitcast.178), channel_id=1, source_target_pairs={{0,1},{1,0},{2,3},{3,2},{4,5},{5,4},{6,7},{7,6},{8,9},{9,8},{10,11... | collective-permute-start | bytes 2359304 | tf_op jit(solution)/shard_map/ppermute | solution.py:24
  34.1 162.3 %collective-permute-start.36 = (bf16[1536,128]{1,0:T(8,128)(2,1)}, bf16[1536,128]{1,0:T(8,128)(2,1)}, u32[]{:S(2)}, u32[]{:S(2)}) collective-permute-start(bf16[1536,128]{1,0:T(8,128)(2,1)} %pad_maximum_fusion.1), channel_id=1, source_target_pairs={{0,1},{1,0},{2,3},{3,2},{4,5},{5,4},{6,7},{7,6},{8,9},{9,8},{10,11... | collective-permute-start | bytes 1179656 | tf_op jit(solution)/shard_map/ppermute | solution.py:24
  113.9 52.3 %collective-permute-start.10 = (bf16[128,1536]{1,0:T(8,128)(2,1)}, bf16[128,1536]{1,0:T(8,128)(2,1)S(1)}, u32[]{:S(2)}, u32[]{:S(2)}) collective-permute-start(bf16[128,1536]{1,0:T(8,128)(2,1)} %dynamic-slice.2), channel_id=1, source_target_pairs={{0,96},{16,112},{32,0},{48,16},{64,32},{80,48},{96,64},{112,80},{1... | collective-permute-start | bytes 1179656 | tf_op jit(solution)/shard_map/ppermute | solution.py:20
  137.4 11.3 %collective-permute-start.5 = (bf16[256,128]{1,0:T(8,128)(2,1)}, bf16[256,128]{1,0:T(8,128)(2,1)}, u32[]{:S(2)}, u32[]{:S(2)}) collective-permute-start(bf16[256,128]{1,0:T(8,128)(2,1)} %fusion.40), channel_id=1, source_target_pairs={{0,1},{1,0},{2,3},{3,2},{4,5},{5,4},{6,7},{7,6},{8,9},{9,8},{10,11... | collective-permute-start | bytes 196616 | tf_op jit(solution)/shard_map/ppermute | solution.py:24
  146.7 20.6 %collective-permute-start.16 = (bf16[128,1536]{1,0:T(8,128)(2,1)}, bf16[128,1536]{1,0:T(8,128)(2,1)}, u32[]{:S(2)}, u32[]{:S(2)}) collective-permute-start(bf16[128,1536]{1,0:T(8,128)(2,1)} %copy.88), channel_id=1, source_target_pairs={{0,96},{16,112},{32,0},{48,16},{64,32},{80,48},{96,64},{112,80},{1... | collective-permute-start | bytes 1179656 | tf_op jit(solution)/shard_map/ppermute | solution.py:20
  146.8 24.2 %collective-permute-start.18 = (bf16[128,1536]{1,0:T(8,128)(2,1)}, bf16[128,1536]{1,0:T(8,128)(2,1)}, u32[]{:S(2)}, u32[]{:S(2)}) collective-permute-start(bf16[128,1536]{1,0:T(8,128)(2,1)} %copy.89), channel_id=1, source_target_pairs={{0,32},{16,48},{32,64},{48,80},{64,96},{80,112},{96,0},{112,16},{1... | collective-permute-start | bytes 1179656 | tf_op jit(solution)/shard_map/ppermute | solution.py:20
  150.8 4.8 %collective-permute-start.38 = (bf16[128,128]{1,0:T(8,128)(2,1)}, bf16[128,128]{1,0:T(8,128)(2,1)}, u32[]{:S(2)}, u32[]{:S(2)}) collective-permute-start(bf16[128,128]{1,0:T(8,128)(2,1)} %slice.159), channel_id=1, source_target_pairs={{0,96},{16,112},{32,0},{48,16},{64,32},{80,48},{96,64},{112,80},{1... | collective-permute-start | bytes 98312 | tf_op jit(solution)/shard_map/ppermute | solution.py:20
  157.2 5.4 %collective-permute-start.40 = (bf16[128,128]{1,0:T(8,128)(2,1)}, bf16[128,128]{1,0:T(8,128)(2,1)}, u32[]{:S(2)}, u32[]{:S(2)}) collective-permute-start(bf16[128,128]{1,0:T(8,128)(2,1)} %get-tuple-element.109), channel_id=1, source_target_pairs={{0,32},{16,48},{32,64},{48,80},{64,96},{80,112},{96,0},{112,16},{1... | collective-permute-start | bytes 98312 | tf_op jit(solution)/shard_map/ppermute | solution.py:20
  162.6 18.6 %collective-permute-start.4 = (bf16[256,1536]{1,0:T(8,128)(2,1)}, bf16[256,1536]{1,0:T(8,128)(2,1)S(1)}, u32[]{:S(2)}, u32[]{:S(2)}) collective-permute-start(bf16[256,1536]{1,0:T(8,128)(2,1)} %dynamic-slice_convert_fusion), channel_id=1, source_target_pairs={{0,1},{1,0},{2,3},{3,2},{4,5},{5,4},{6,7},{7,6},{8,9},{9,8},{10,11... | collective-permute-start | bytes 2359304 | tf_op jit(solution)/shard_map/ppermute | solution.py:24
  166.2 29.5 %collective-permute-start.37 = (bf16[256,128]{1,0:T(8,128)(2,1)}, bf16[256,128]{1,0:T(8,128)(2,1)}, u32[]{:S(2)}, u32[]{:S(2)}) collective-permute-start(bf16[256,128]{1,0:T(8,128)(2,1)} %copy-done.20), channel_id=1, source_target_pairs={{0,16},{16,0},{32,48},{48,32},{64,80},{80,64},{96,112},{112,96},{1... | collective-permute-start | bytes 196616 | tf_op jit(solution)/shard_map/ppermute | solution.py:24
  167.3 18.8 %collective-permute-start.39 = (bf16[128,128]{1,0:T(8,128)(2,1)}, bf16[128,128]{1,0:T(8,128)(2,1)}, u32[]{:S(2)}, u32[]{:S(2)}) collective-permute-start(bf16[128,128]{1,0:T(8,128)(2,1)} %get-tuple-element.108), channel_id=1, source_target_pairs={{0,96},{16,112},{32,0},{48,16},{64,32},{80,48},{96,64},{112,80},{1... | collective-permute-start | bytes 98312 | tf_op jit(solution)/shard_map/ppermute | solution.py:20
  171.0 26.9 %collective-permute-start.11 = (bf16[128,1536]{1,0:T(8,128)(2,1)}, bf16[128,1536]{1,0:T(8,128)(2,1)}, u32[]{:S(2)}, u32[]{:S(2)}) collective-permute-start(bf16[128,1536]{1,0:T(8,128)(2,1)} %get-tuple-element.86), channel_id=1, source_target_pairs={{0,96},{16,112},{32,0},{48,16},{64,32},{80,48},{96,64},{112,80},{1... | collective-permute-start | bytes 1179656 | tf_op jit(solution)/shard_map/ppermute | solution.py:20
  181.2 19.9 %collective-permute-start.12 = (bf16[128,1536]{1,0:T(8,128)(2,1)}, bf16[128,1536]{1,0:T(8,128)(2,1)S(1)}, u32[]{:S(2)}, u32[]{:S(2)}) collective-permute-start(bf16[128,1536]{1,0:T(8,128)(2,1)} %get-tuple-element.87), channel_id=1, source_target_pairs={{0,32},{16,48},{32,64},{48,80},{64,96},{80,112},{96,0},{112,16},{1... | collective-permute-start | bytes 1179656 | tf_op jit(solution)/shard_map/ppermute | solution.py:20
  186.0 9.8 %collective-permute-start.41 = (bf16[128,128]{1,0:T(8,128)(2,1)}, bf16[128,128]{1,0:T(8,128)(2,1)S(1)}, u32[]{:S(2)}, u32[]{:S(2)}) collective-permute-start(bf16[128,128]{1,0:T(8,128)(2,1)} %broadcast_select_fusion.10), channel_id=1, source_target_pairs={{0,32},{16,48},{32,64},{48,80},{64,96},{80,112},{96,0},{112,16},{1... | collective-permute-start | bytes 98312 | tf_op jit(solution)/shard_map/ppermute | solution.py:20
  188.6 14.7 %all-to-all-start = ((f32[16,1,1]{2,1,0:T(1,128)}), f32[16,1,1]{2,1,0:T(1,128)}, u32[]{:S(2)}, u32[]{:S(2)}) async-start(f32[16,1,1]{2,1,0:T(1,128)} %broadcast_in_dim.66), calls=%async_computation | async-start | bytes 16384 | tf_op jit(solution)/shard_map/all_to_all | solution.py:35
  195.7 258.7 %collective-permute-start.8 = (bf16[3072,1536]{1,0:T(8,128)(2,1)}, bf16[3072,1536]{1,0:T(8,128)(2,1)}, u32[]{:S(2)}, u32[]{:S(2)}) collective-permute-start(bf16[3072,1536]{1,0:T(8,128)(2,1)} %bitcast.173), channel_id=1, source_target_pairs={{0,16},{16,0},{32,48},{48,32},{64,80},{80,64},{96,112},{112,96},{1... | collective-permute-start | bytes 28311560 | tf_op jit(solution)/shard_map/ppermute | solution.py:24
  195.8 22.9 %collective-permute-start.9 = (bf16[256,1536]{1,0:T(8,128)(2,1)S(1)}, bf16[256,1536]{1,0:T(8,128)(2,1)}, u32[]{:S(2)}, u32[]{:S(2)}) collective-permute-start(bf16[256,1536]{1,0:T(8,128)(2,1)S(1)} %copy-done.12), channel_id=1, source_target_pairs={{0,16},{16,0},{32,48},{48,32},{64,80},{80,64},{96,112},{112,96},{1... | collective-permute-start | bytes 2359304 | tf_op jit(solution)/shard_map/ppermute | solution.py:24
  196.4 22.2 %collective-permute-start.2 = (bf16[256,1536]{1,0:T(8,128)(2,1)}, bf16[256,1536]{1,0:T(8,128)(2,1)S(1)}, u32[]{:S(2)}, u32[]{:S(2)}) collective-permute-start(bf16[256,1536]{1,0:T(8,128)(2,1)} %add_convert_fusion.1), channel_id=1, source_target_pairs={{0,2},{2,4},{4,6},{6,8},{8,10},{10,12},{12,14},{14,0},{1,3},{3,5},... | collective-permute-start | bytes 2359304 | tf_op jit(solution)/shard_map/ppermute | solution.py:20
  197.9 22.1 %collective-permute-start.17 = (bf16[128,1536]{1,0:T(8,128)(2,1)}, bf16[128,1536]{1,0:T(8,128)(2,1)}, u32[]{:S(2)}, u32[]{:S(2)}) collective-permute-start(bf16[128,1536]{1,0:T(8,128)(2,1)} %broadcast_select_fusion.5), channel_id=1, source_target_pairs={{0,96},{16,112},{32,0},{48,16},{64,32},{80,48},{96,64},{112,80},{1... | collective-permute-start | bytes 1179656 | tf_op jit(solution)/shard_map/ppermute | solution.py:20
  201.1 20.3 %collective-permute-start.19 = (bf16[128,1536]{1,0:T(8,128)(2,1)}, bf16[128,1536]{1,0:T(8,128)(2,1)}, u32[]{:S(2)}, u32[]{:S(2)}) collective-permute-start(bf16[128,1536]{1,0:T(8,128)(2,1)} %broadcast_select_fusion.4), channel_id=1, source_target_pairs={{0,32},{16,48},{32,64},{48,80},{64,96},{80,112},{96,0},{112,16},{1... | collective-permute-start | bytes 1179656 | tf_op jit(solution)/shard_map/ppermute | solution.py:20
  218.7 13.1 %collective-permute-start.15 = (bf16[256,1536]{1,0:T(8,128)(2,1)}, bf16[256,1536]{1,0:T(8,128)(2,1)}, u32[]{:S(2)}, u32[]{:S(2)}) collective-permute-start(bf16[256,1536]{1,0:T(8,128)(2,1)} %copy.87), channel_id=1, source_target_pairs={{0,16},{16,0},{32,48},{48,32},{64,80},{80,64},{96,112},{112,96},{1... | collective-permute-start | bytes 2359304 | tf_op jit(solution)/shard_map/ppermute | solution.py:24
  218.7 16.4 %collective-permute-start.13 = (bf16[128,1536]{1,0:T(8,128)(2,1)}, bf16[128,1536]{1,0:T(8,128)(2,1)}, u32[]{:S(2)}, u32[]{:S(2)}) collective-permute-start(bf16[128,1536]{1,0:T(8,128)(2,1)} %broadcast_select_fusion.6), channel_id=1, source_target_pairs={{0,32},{16,48},{32,64},{48,80},{64,96},{80,112},{96,0},{112,16},{1... | collective-permute-start | bytes 1179656 | tf_op jit(solution)/shard_map/ppermute | solution.py:20
  220.0 11.9 %collective-permute-start.6 = (f32[2,256]{1,0:T(2,128)}, f32[2,256]{1,0:T(2,128)}, u32[]{:S(2)}, u32[]{:S(2)}) collective-permute-start(f32[2,256]{1,0:T(2,128)} %pad_maximum_fusion.2), channel_id=1, source_target_pairs={{0,1},{1,0},{2,3},{3,2},{4,5},{5,4},{6,7},{7,6},{8,9},{9,8},{10,11... | collective-permute-start | bytes 6152 | tf_op jit(solution)/shard_map/ppermute | solution.py:24
  221.5 13.7 %collective-permute-start.22 = (f32[1664]{0:T(1024)}, f32[1664]{0:T(1024)}, u32[]{:S(2)}, u32[]{:S(2)}) collective-permute-start(f32[1664]{0:T(1024)} %concatenate.80), channel_id=1, source_target_pairs={{0,64},{16,80},{32,96},{48,112},{64,0},{80,16},{96,32},{112,48},{1... | collective-permute-start | bytes 19976 | tf_op jit(solution)/shard_map/ppermute | solution.py:24
  231.8 55.7 %collective-permute-start.28 = (bf16[768,1536]{1,0:T(8,128)(2,1)}, bf16[768,1536]{1,0:T(8,128)(2,1)}, u32[]{:S(2)}, u32[]{:S(2)}) collective-permute-start(bf16[768,1536]{1,0:T(8,128)(2,1)} %get-tuple-element.94), channel_id=1, source_target_pairs={{0,32},{16,48},{32,64},{48,80},{64,96},{80,112},{96,0},{112,16},{1... | collective-permute-start | bytes 7077896 | tf_op jit(solution)/shard_map/ppermute | solution.py:20
  231.9 55.6 %collective-permute-start.23 = (bf16[768,1536]{1,0:T(8,128)(2,1)}, bf16[768,1536]{1,0:T(8,128)(2,1)}, u32[]{:S(2)}, u32[]{:S(2)}) collective-permute-start(bf16[768,1536]{1,0:T(8,128)(2,1)} %get-tuple-element.95), channel_id=1, source_target_pairs={{0,96},{16,112},{32,0},{48,16},{64,32},{80,48},{96,64},{112,80},{1... | collective-permute-start | bytes 7077896 | tf_op jit(solution)/shard_map/ppermute | solution.py:20
  235.1 101.7 %collective-permute-start.27 = (bf16[768,1536]{1,0:T(8,128)(2,1)}, bf16[768,1536]{1,0:T(8,128)(2,1)}, u32[]{:S(2)}, u32[]{:S(2)}) collective-permute-start(bf16[768,1536]{1,0:T(8,128)(2,1)} %get-tuple-element.96), channel_id=1, source_target_pairs={{0,32},{16,48},{32,64},{48,80},{64,96},{80,112},{96,0},{112,16},{1... | collective-permute-start | bytes 7077896 | tf_op jit(solution)/shard_map/ppermute | solution.py:20
  235.1 101.7 %collective-permute-start.25 = (bf16[768,1536]{1,0:T(8,128)(2,1)}, bf16[768,1536]{1,0:T(8,128)(2,1)}, u32[]{:S(2)}, u32[]{:S(2)}) collective-permute-start(bf16[768,1536]{1,0:T(8,128)(2,1)} %get-tuple-element.97), channel_id=1, source_target_pairs={{0,96},{16,112},{32,0},{48,16},{64,32},{80,48},{96,64},{112,80},{1... | collective-permute-start | bytes 7077896 | tf_op jit(solution)/shard_map/ppermute | solution.py:20
  247.3 112.2 %slice-start.3 = ((s8[9437184]{0:T(1024)(128)(4,1)}), s8[4194304]{0:T(1024)(128)(4,1)S(1)}, s32[]{:S(2)}) async-start(s8[9437184]{0:T(1024)(128)(4,1)} %bitcast.176), calls=%async_computation.4 | async-start | bytes 8388608
  247.5 112.0 %slice-start.4 = ((s8[9437184]{0:T(1024)(128)(4,1)}), s8[4194304]{0:T(1024)(128)(4,1)S(1)}, s32[]{:S(2)}) async-start(s8[9437184]{0:T(1024)(128)(4,1)} %bitcast.176), calls=%async_computation.5 | async-start | bytes 8388608
  247.5 112.0 %slice-start.5 = ((s8[9437184]{0:T(1024)(128)(4,1)}), s8[1048576]{0:T(1024)(128)(4,1)S(1)}, s32[]{:S(2)}) async-start(s8[9437184]{0:T(1024)(128)(4,1)} %bitcast.176), calls=%async_computation.6 | async-start | bytes 2097152
  287.5 63.3 %collective-permute-start.21 = (f32[1664]{0:T(1024)}, f32[1664]{0:T(1024)S(1)}, u32[]{:S(2)}, u32[]{:S(2)}) collective-permute-start(f32[1664]{0:T(1024)} %concatenate.80), channel_id=1, source_target_pairs={{0,32},{16,48},{32,0},{48,16},{64,96},{80,112},{96,64},{112,80},{1... | collective-permute-start | bytes 19976 | tf_op jit(solution)/shard_map/ppermute | solution.py:24
  287.5 63.3 %collective-permute-start.20 = (f32[1664]{0:T(1024)}, f32[1664]{0:T(1024)S(1)}, u32[]{:S(2)}, u32[]{:S(2)}) collective-permute-start(f32[1664]{0:T(1024)} %concatenate.80), channel_id=1, source_target_pairs={{0,16},{16,0},{32,48},{48,32},{64,80},{80,64},{96,112},{112,96},{1... | collective-permute-start | bytes 19976 | tf_op jit(solution)/shard_map/ppermute | solution.py:24
  336.8 18.3 %collective-permute-start.7 = (bf16[256,1536]{1,0:T(8,128)(2,1)S(1)}, bf16[256,1536]{1,0:T(8,128)(2,1)S(1)}, u32[]{:S(2)}, u32[]{:S(2)}) collective-permute-start(bf16[256,1536]{1,0:T(8,128)(2,1)S(1)} %fusion.26), channel_id=1, source_target_pairs={{0,14},{2,0},{4,2},{6,4},{8,6},{10,8},{12,10},{14,12},{1,15},{3,1}... | collective-permute-start | bytes 2359304 | tf_op jit(solution)/shard_map/ppermute | solution.py:20
  336.8 19.8 %collective-permute-start.14 = (bf16[256,1536]{1,0:T(8,128)(2,1)S(1)}, bf16[256,1536]{1,0:T(8,128)(2,1)S(1)}, u32[]{:S(2)}, u32[]{:S(2)}) collective-permute-start(bf16[256,1536]{1,0:T(8,128)(2,1)S(1)} %pad_maximum_fusion), channel_id=1, source_target_pairs={{0,1},{1,0},{2,3},{3,2},{4,5},{5,4},{6,7},{7,6},{8,9},{9,8},{10,11... | collective-permute-start | bytes 2359304 | tf_op jit(solution)/shard_map/ppermute | solution.py:24
  350.8 55.7 %collective-permute-start.30 = (bf16[768,1536]{1,0:T(8,128)(2,1)}, bf16[768,1536]{1,0:T(8,128)(2,1)}, u32[]{:S(2)}, u32[]{:S(2)}) collective-permute-start(bf16[768,1536]{1,0:T(8,128)(2,1)} %get-tuple-element.90), channel_id=1, source_target_pairs={{0,32},{16,48},{32,64},{48,80},{64,96},{80,112},{96,0},{112,16},{1... | collective-permute-start | bytes 7077896 | tf_op jit(solution)/shard_map/ppermute | solution.py:20
  350.9 103.5 %collective-permute-start.26 = (bf16[768,1536]{1,0:T(8,128)(2,1)}, bf16[768,1536]{1,0:T(8,128)(2,1)}, u32[]{:S(2)}, u32[]{:S(2)}) collective-permute-start(bf16[768,1536]{1,0:T(8,128)(2,1)} %get-tuple-element.91), channel_id=1, source_target_pairs={{0,96},{16,112},{32,0},{48,16},{64,32},{80,48},{96,64},{112,80},{1... | collective-permute-start | bytes 7077896 | tf_op jit(solution)/shard_map/ppermute | solution.py:20
  355.1 99.3 %collective-permute-start.29 = (bf16[768,1536]{1,0:T(8,128)(2,1)}, bf16[768,1536]{1,0:T(8,128)(2,1)}, u32[]{:S(2)}, u32[]{:S(2)}) collective-permute-start(bf16[768,1536]{1,0:T(8,128)(2,1)} %get-tuple-element.92), channel_id=1, source_target_pairs={{0,32},{16,48},{32,64},{48,80},{64,96},{80,112},{96,0},{112,16},{1... | collective-permute-start | bytes 7077896 | tf_op jit(solution)/shard_map/ppermute | solution.py:20
  356.6 97.8 %collective-permute-start.24 = (bf16[768,1536]{1,0:T(8,128)(2,1)}, bf16[768,1536]{1,0:T(8,128)(2,1)}, u32[]{:S(2)}, u32[]{:S(2)}) collective-permute-start(bf16[768,1536]{1,0:T(8,128)(2,1)} %get-tuple-element.93), channel_id=1, source_target_pairs={{0,96},{16,112},{32,0},{48,16},{64,32},{80,48},{96,64},{112,80},{1... | collective-permute-start | bytes 7077896 | tf_op jit(solution)/shard_map/ppermute | solution.py:20
  (39 other events, 431.6 us)
